TPU v7x, 128 devices: a whole 4x4x4 slice. The times are simulated.
128 devices in a mesh: row: 8 (over z, core), col: 16 (over y, x).
Axes of the slice: x: 4, y: 4, z: 4, core: 2. Of those that a mesh axis runs over, the one named last changes fastest.
Arguments:
- kernel: float32 [16384, 16384], P('row', 'col'), may hold values from 0 to 3, as said below
Outputs:
- trailing: float32 [16384, 16384], P('row', 'col')
- factor_t: float32 [1024, 16384], P('col', 'row')
Inputs may be any that keep to these rules, and one draw needn't show every extreme that they name: K is symmetric: an RBF kernel over 256 donor features plus each donor's noise variance, of 0.5 or more, on the diagonal.
All inputs are finite; a program needn't handle non-finite values.
Results may differ from a plain program's by a relative error of at most 0.0003.
Values sent between devices are 32-bit elements; how exact they have to be, the bound alone decides.
A program may use at most 128 MiB of HBM per device.

v0:
```python
import jax
import jax.numpy as jnp
from jax import lax
from jax.sharding import PartitionSpec as P

PANEL = 512
PANELS = 2
TILE = 32
HIGHEST = lax.Precision.HIGHEST


def mm(a, b):
    return jnp.dot(a, b, precision=HIGHEST, preferred_element_type=jnp.float32)


def mm_tn(a, b):
    return lax.dot_general(
        a, b, (((0,), (0,)), ((), ())), precision=HIGHEST, preferred_element_type=jnp.float32
    )


def mm_nt(a, b):
    return lax.dot_general(
        a, b, (((1,), (1,)), ((), ())), precision=HIGHEST, preferred_element_type=jnp.float32
    )


def tri_inverse(lower):
    eye = jnp.eye(lower.shape[0], dtype=lower.dtype)
    return jax.scipy.linalg.solve_triangular(lower, eye, lower=True)


def sym_chol(block):
    return jnp.linalg.cholesky(block)


def local(kernel):
    grid_rows = lax.axis_size("row")
    grid_cols = lax.axis_size("col")
    my_row = lax.axis_index("row")
    my_col = lax.axis_index("col")
    rows_loc, cols_loc = kernel.shape
    lead = PANELS * PANEL
    lead_rt = lead // (TILE * grid_rows)
    lead_ct = lead // (TILE * grid_cols)
    lead_r = lead_rt * TILE
    lead_c = lead_ct * TILE
    row_local = jnp.arange(rows_loc, dtype=jnp.int32)
    row_ids = (row_local // TILE * grid_rows + my_row) * TILE + row_local % TILE
    col_local = jnp.arange(cols_loc, dtype=jnp.int32)
    col_ids = (col_local // TILE * grid_cols + my_col) * TILE + col_local % TILE
    corner = kernel[:lead_r, :lead_c].reshape(1, lead_r * lead_c)
    blocks = lax.all_gather(corner, ("row", "col"), axis=0, tiled=True)
    blocks = blocks.reshape(grid_rows, grid_cols, lead_rt, TILE, lead_ct, TILE)
    a_lead = blocks.transpose(2, 0, 3, 4, 1, 5).reshape(lead, lead)
    cols_part = lax.all_gather(kernel[:, :lead_c], "col", axis=1, tiled=True)
    cols_part = cols_part.reshape(rows_loc, grid_cols, lead_ct, TILE)
    x_rows = cols_part.transpose(0, 2, 1, 3).reshape(rows_loc, lead)
    rows_part = lax.all_gather(kernel[:lead_r, :], "row", axis=0, tiled=True)
    rows_part = rows_part.reshape(grid_rows, lead_rt, TILE, cols_loc)
    y_cols = rows_part.transpose(1, 0, 2, 3).reshape(lead, cols_loc)
    a00 = a_lead[:PANEL, :PANEL]
    a01 = a_lead[:PANEL, PANEL:]
    a11 = a_lead[PANEL:, PANEL:]
    l0 = sym_chol(a00)
    l0inv = tri_inverse(l0)
    g0p1 = mm(l0inv, a01)
    s11 = a11 - mm_tn(g0p1, g0p1)
    l1 = sym_chol(s11)
    l1inv = tri_inverse(l1)

    def factor(panel_t, ids):
        g0 = mm(l0inv, panel_t[:PANEL])
        s1 = panel_t[PANEL:] - mm_tn(g0p1, g0)
        g1 = mm(l1inv, s1)
        g1 = jnp.where(ids[None, :] >= PANEL, g1, 0.0)
        return jnp.concatenate([g0, g1], axis=0)

    g_rows = factor(x_rows.T, row_ids)
    g_cols = factor(y_cols, col_ids)
    schur = kernel - mm_tn(g_rows, g_cols)
    keep = (row_ids[:, None] >= lead) & (col_ids[None, :] >= lead)
    trailing = jnp.where(keep, schur, 0.0)
    per_col = lead // grid_cols
    factor_out = lax.dynamic_slice_in_dim(g_rows, my_col * per_col, per_col, 0)
    return (trailing, factor_out)


def solution(mesh):
    return jax.shard_map(
        local,
        mesh=mesh,
        in_specs=(P("row", "col"),),
        out_specs=(P("row", "col"), P("col", "row")),
        check_vma=False,
    )
```

profile of v0, /device:TPU:1, one launch (start us, length us, event | category | flops | bytes accessed | tf_op | source)
XLA Modules:
  0.0 584.9 jit_solution(12073595241916444088)
XLA Ops:
  7.2 2.0 slice.123
  12.2 34.1 %all-gather.7.cloned.1.call-done = f32[1024,1024]{1,0:T(8,128)} async-done(((f32[128,1024]{1,0:T(8,128)}), f32[1024,1024]{1,0:T(8,128)}) %all-gather.7.cloned.1.call-update) | async-done | bytes 4194320 | tf_op jit(solution)/shard_map/all_gather | solution.py:59
  46.3 2.5 fusion.105
  51.7 65.0 %all-gather.9.cloned.1.call-done = f32[128,1,8192]{2,1,0:T(1,128)} async-done(((f32[1,1,8192]{2,1,0:T(1,128)}), f32[128,1,8192]{2,1,0:T(1,128)}) %all-gather.9.cloned.1.call-update) | async-done | bytes 4194320 | tf_op jit(solution)/shard_map/all_gather | solution.py:53
  116.7 13.2 %reduce.16 = f32[128,8192]{1,0:T(8,128)} reduce(f32[128,1,8192]{2,1,0:T(1,128)} %all-gather.9.cloned.1.call-done, f32[]{:T(128)} %constant.211), dimensions={1}, to_apply=%all-gather.reduce_sub_computation | reduce | bytes 8388612 | tf_op jit(solution)/shard_map/all_gather | solution.py:53
  129.9 16.6 %reshape.139 = f32[8,16,4,32,2,32]{5,4,3,2,1,0:T(2,128)} reshape(f32[128,8192]{1,0:T(8,128)} %reduce.16) | data formatting | bytes 8388608 | tf_op jit(solution)/shard_map/reshape | solution.py:54
  146.5 26.1 %copy.20 = f32[4,8,32,2,16,32]{2,1,0,5,4,3:T(8,128)} copy(f32[4,8,32,2,16,32]{5,3,2,0,4,1:T(2,128)} %bitcast.121) | data formatting | bytes 8388608 | tf_op jit(solution)/shard_map/transpose | solution.py:55
  172.6 14.3 %reshape.140 = f32[1024,1024]{0,1:T(8,128)} reshape(f32[4,8,32,2,16,32]{2,1,0,5,4,3:T(8,128)} %copy.20) | data formatting | bytes 8388608 | tf_op jit(solution)/shard_map/reshape | solution.py:55
  186.9 2.3 slice.141
  193.2 11.7 %cholesky.286 = f32[128,128]{1,0:T(8,128)S(1)} custom-call(f32[128,128]{1,0:T(8,128)S(1)} %cholesky.426), custom_call_target="Cholesky" | custom-call | tf_op jit(solution)/shard_map/jit(cholesky)/cholesky | solution.py:34
  204.9 9.8 %custom-call.27 = f32[1,128,128]{1,2,0:T(8,128)S(1)} custom-call(f32[1,128,128]{2,1,0:T(8,128)S(1)} %get-tuple-element.61), custom_call_target="InvertDiagBlocksLowerTriangular" | custom-call | tf_op jit(solution)/shard_map/jit(cholesky)/cholesky | solution.py:34
  217.4 11.7 %cholesky.305 = f32[128,128]{1,0:T(8,128)S(1)} custom-call(f32[128,128]{1,0:T(8,128)S(1)} %cholesky.430), custom_call_target="Cholesky" | custom-call | tf_op jit(solution)/shard_map/jit(cholesky)/cholesky | solution.py:34
  229.1 10.0 %custom-call.28 = f32[1,128,128]{1,2,0:T(8,128)S(1)} custom-call(f32[1,128,128]{2,1,0:T(8,128)S(1)} %get-tuple-element.58), custom_call_target="InvertDiagBlocksLowerTriangular" | custom-call | tf_op jit(solution)/shard_map/jit(cholesky)/cholesky | solution.py:34
  240.7 11.7 %cholesky.326 = f32[128,128]{1,0:T(8,128)S(1)} custom-call(f32[128,128]{1,0:T(8,128)S(1)} %cholesky.435), custom_call_target="Cholesky" | custom-call | tf_op jit(solution)/shard_map/jit(cholesky)/cholesky | solution.py:34
  252.4 9.8 %custom-call.29 = f32[1,128,128]{1,2,0:T(8,128)S(1)} custom-call(f32[1,128,128]{2,1,0:T(8,128)S(1)} %get-tuple-element.55), custom_call_target="InvertDiagBlocksLowerTriangular" | custom-call | tf_op jit(solution)/shard_map/jit(cholesky)/cholesky | solution.py:34
  263.7 11.7 %cholesky.343 = f32[128,128]{1,0:T(8,128)S(1)} custom-call(f32[128,128]{1,0:T(8,128)S(1)} %convolution_subtract_fusion.12), custom_call_target="Cholesky" | custom-call | tf_op jit(solution)/shard_map/jit(cholesky)/cholesky | solution.py:34
  281.6 12.0 %while.4 = (s32[]{:T(128)}, f32[512,512]{1,0:T(8,128)}, s32[4,2]{0,1:T(2,128)S(1)}, f32[4,128,128]{2,1,0:T(8,128)S(1)}, s32[]{:T(128)}) while((s32[]{:T(128)}, f32[512,512]{1,0:T(8,128)}, s32[4,2]{0,1:T(2,128)S(1)}, f32[4,128,128]{2,1,0:T(8,128)S(1)}, s32[]{:T(128)}) %tuple.58), condition=%wide.while_cond, body=%wide.while_body.sunk | while | flops 2 | bytes 131181 | solution.py:30
  282.3 2.3 bitcast_dynamic-update-slice_fusion.4
  285.3 2.3 bitcast_dynamic-update-slice_fusion.4
  288.4 2.3 bitcast_dynamic-update-slice_fusion.4
  291.4 2.3 bitcast_dynamic-update-slice_fusion.4
  293.7 39.3 %custom-call.30 = f32[4,128,128]{1,2,0:T(8,128)S(1)} custom-call(f32[4,128,128]{2,1,0:T(8,128)S(1)} %get-tuple-element.18), custom_call_target="InvertDiagBlocksLowerTriangular" | custom-call | tf_op jit(solution)/shard_map/jit(_solve_triangular)/triangular_solve | solution.py:30
  339.1 1.9 fusion.10
  340.9 2.9 convolution_subtract_fusion
  343.8 2.5 copy.25
  349.1 11.7 %cholesky.358 = f32[128,128]{1,0:T(8,128)S(1)} custom-call(f32[128,128]{1,0:T(8,128)S(1)} %cholesky.439), custom_call_target="Cholesky" | custom-call | tf_op jit(solution)/shard_map/jit(cholesky)/cholesky | solution.py:34
  362.0 10.0 %custom-call.31 = f32[1,128,128]{1,2,0:T(8,128)S(1)} custom-call(f32[1,128,128]{2,1,0:T(8,128)S(1)} %get-tuple-element.51), custom_call_target="InvertDiagBlocksLowerTriangular" | custom-call | tf_op jit(solution)/shard_map/jit(cholesky)/cholesky | solution.py:34
  372.0 1.9 constant_dynamic-update-slice_fusion.3
  375.1 11.7 %cholesky.377 = f32[128,128]{1,0:T(8,128)S(1)} custom-call(f32[128,128]{1,0:T(8,128)S(1)} %cholesky.443), custom_call_target="Cholesky" | custom-call | tf_op jit(solution)/shard_map/jit(cholesky)/cholesky | solution.py:34
  387.5 9.8 %custom-call.32 = f32[1,128,128]{1,2,0:T(8,128)S(1)} custom-call(f32[1,128,128]{2,1,0:T(8,128)S(1)} %get-tuple-element.48), custom_call_target="InvertDiagBlocksLowerTriangular" | custom-call | tf_op jit(solution)/shard_map/jit(cholesky)/cholesky | solution.py:34
  399.7 11.7 %cholesky.398 = f32[128,128]{1,0:T(8,128)S(1)} custom-call(f32[128,128]{1,0:T(8,128)S(1)} %cholesky.448), custom_call_target="Cholesky" | custom-call | tf_op jit(solution)/shard_map/jit(cholesky)/cholesky | solution.py:34
  412.0 10.0 %custom-call.33 = f32[1,128,128]{1,2,0:T(8,128)S(1)} custom-call(f32[1,128,128]{2,1,0:T(8,128)S(1)} %get-tuple-element.45), custom_call_target="InvertDiagBlocksLowerTriangular" | custom-call | tf_op jit(solution)/shard_map/jit(cholesky)/cholesky | solution.py:34
  424.3 11.7 %cholesky.415 = f32[128,128]{1,0:T(8,128)S(1)} custom-call(f32[128,128]{1,0:T(8,128)S(1)} %convolution_subtract_fusion.11), custom_call_target="Cholesky" | custom-call | tf_op jit(solution)/shard_map/jit(cholesky)/cholesky | solution.py:34
  442.0 2.3 select_select_fusion
  444.4 11.7 %while.5 = (s32[]{:T(128)}, f32[512,512]{1,0:T(8,128)}, s32[4,2]{0,1:T(2,128)S(1)}, f32[4,128,128]{2,1,0:T(8,128)S(1)}, s32[]{:T(128)}) while((s32[]{:T(128)}, f32[512,512]{1,0:T(8,128)}, s32[4,2]{0,1:T(2,128)S(1)}, f32[4,128,128]{2,1,0:T(8,128)S(1)}, s32[]{:T(128)}) %tuple.70), condition=%wide.while_cond.clone, body=%wide.while_body.clone.sunk | while | flops 2 | bytes 131181 | solution.py:30
  445.1 2.2 bitcast_dynamic-update-slice_fusion.5
  448.0 2.2 bitcast_dynamic-update-slice_fusion.5
  451.0 2.2 bitcast_dynamic-update-slice_fusion.5
  453.9 2.2 bitcast_dynamic-update-slice_fusion.5
  456.1 39.7 %custom-call.34 = f32[4,128,128]{1,2,0:T(8,128)S(1)} custom-call(f32[4,128,128]{2,1,0:T(8,128)S(1)} %get-tuple-element.19), custom_call_target="InvertDiagBlocksLowerTriangular" | custom-call | tf_op jit(solution)/shard_map/jit(_solve_triangular)/triangular_solve | solution.py:30
  504.8 4.5 fusion.46
  509.3 3.5 bitcast_subtract_fusion
  512.9 5.1 convolution_select_fusion
  517.9 4.0 copy.23
  521.9 7.2 %fusion.2 = f32[512,2048]{1,0:T(8,128)S(1)} fusion(f32[1024,2048]{1,0:T(8,128)S(1)} %bitcast.122, f32[128,512]{1,0:T(8,128)S(1)} %copy-done.8, f32[128,512]{1,0:T(8,128)S(1)} %fusion.60, f32[128,512]{1,0:T(8,128)S(1)} %fusion.62, f32[128,512]{1,0:T(8,128)S(1)} %fusion.36), kind=kOutput, calls=%fused_computation.11 | convolution fusion | flops 6443237376 | bytes 9437184 | tf_op jit(solution)/shard_map/dot_general | solution.py:13
  529.1 7.7 %fusion.106 = f32[512,2048]{1,0:T(8,128)S(1)} fusion(f32[512,512]{1,0:T(8,128)S(1)} %fusion.10, f32[512,2048]{1,0:T(8,128)S(1)} %fusion.2), kind=kOutput, calls=%fused_computation.193 | convolution fusion | flops 6442450944 | bytes 9437184 | tf_op jit(solution)/shard_map/dot_general | solution.py:17
  536.9 7.2 %fusion.7 = f32[512,2048]{1,0:T(8,128)S(1)} fusion(f32[512,2048]{1,0:T(8,128)S(1)} %fusion.106, f32[1024,2048]{1,0:T(8,128)S(1)} %bitcast.123, pred[2048]{0:T(1024)(128)(4,1)S(1)} %get-tuple-element.68, f32[128,512]{1,0:T(8,128)S(1)} %fusion.53, f32[128,512]{1,0:T(8,128)S(1)} %copy-done.6, f32[128,512]{1,0:T(8,128)S(1)} %fusion.56, f32[128,512]{1,0:T(8,128)S(1)} %fusion.34), kind=kOutput, calls=%fused_computation.16 | convolution fusion | flops 6445334528 | bytes 13633536 | tf_op jit(solution)/shard_map/dot_general | solution.py:13
  546.5 31.7 %subtract_select_fusion = f32[2048,1024]{1,0:T(8,128)} fusion(f32[2048,1024]{1,0:T(8,128)} %param.4, pred[1024]{0:T(1024)(128)(4,1)S(1)} %get-tuple-element.67, pred[2048]{0:T(1024)(128)(4,1)S(1)} %get-tuple-element.69, f32[512,1024]{1,0:T(8,128)S(1)} %copy-done.11, f32[512,1024]{1,0:T(8,128)S(1)} %copy-done.3, f32[512,2048]{1,0:T(8,128)S(1)} %fusion.7, ...), kind=kOutput, calls=%fused_computation.8 | convolution fusion | flops 25779240960 | bytes 29363200 | tf_op jit(solution)/shard_map/dot_general | solution.py:17
  (116 shorter events, 56.2 us)
Async XLA Ops:
  7.2 3.7 slice-start
  7.2 39.1 %all-gather.7.cloned.1.call-start = ((), (), s32[]{:S(2)}) async-start(), calls=%async_computation.1 | async-start | bytes 4718592 | tf_op jit(solution)/shard_map/all_gather | solution.py:59
  9.2 107.5 %all-gather.9.cloned.1.call-start = ((), (), s32[]{:S(2)}) async-start(), calls=%async_computation.2 | async-start | bytes 4227072 | tf_op jit(solution)/shard_map/all_gather | solution.py:53
  10.8 507.1 %all-gather.5.cloned.1.call-start = ((), (), s32[]{:S(2)}) async-start(), calls=%async_computation | async-start | bytes 8912896 | tf_op jit(solution)/shard_map/all_gather | solution.py:56
  192.2 1.0 copy-start.10
  333.0 6.0 %copy-start = (f32[1024,1024]{0,1:T(8,128)S(1)}, f32[1024,1024]{0,1:T(8,128)}, u32[]{:S(2)}) copy-start(f32[1024,1024]{0,1:T(8,128)} %reshape.140) | copy-start | bytes 12582916
  339.1 7.3 %copy-start.7 = (f32[128,512]{1,0:T(8,128)}, f32[128,512]{1,0:T(8,128)S(1)}, u32[]{:S(2)}) copy-start(f32[128,512]{1,0:T(8,128)S(1)} %fusion.59) | copy-start | bytes 786436
  348.1 1.0 copy-start.9
  495.8 0.7 copy-start.12
  495.8 8.9 %copy-start.4 = (f32[2,8,32,1024]{3,2,1,0:T(8,128)S(1)}, f32[2,8,32,1024]{3,2,1,0:T(8,128)}, u32[]{:S(2)}) copy-start(f32[2,8,32,1024]{3,2,1,0:T(8,128)} %copy.26) | copy-start | bytes 6291460
  500.4 8.9 %copy-start.1 = (f32[2,8,32,1024]{3,2,1,0:T(8,128)S(1)}, f32[2,8,32,1024]{3,2,1,0:T(8,128)}, u32[]{:S(2)}) copy-start(f32[2,8,32,1024]{3,2,1,0:T(8,128)} %copy.27) | copy-start | bytes 6291460
  501.8 11.1 %copy-start.5 = (f32[128,512]{1,0:T(8,128)}, f32[128,512]{1,0:T(8,128)S(1)}, u32[]{:S(2)}) copy-start(f32[128,512]{1,0:T(8,128)S(1)} %fusion.54) | copy-start | bytes 786436
  509.3 3.5 copy-start.2
  517.9 4.0 copy-start.8
  529.1 7.8 %copy-start.6 = (f32[128,512]{1,0:T(8,128)S(1)}, f32[128,512]{1,0:T(8,128)}, u32[]{:S(2)}) copy-start(f32[128,512]{1,0:T(8,128)} %copy-done.5) | copy-start | bytes 786436
  544.0 1.8 copy-start.3
  544.1 2.4 copy-start.11
Sparse Core Ops, SparseCore 0:
  10.3 35.9 all-gather.6
  50.0 66.6 all-gather.8
  118.9 67.6 all-gather.4
where the time goes:
time: 592 us; the launch traced here: 585 us
  other arithmetic  260 us (44%)
  local copies, waits for them, and re-layouts  106 us (18%)
  matrix products  99.3 us (17%)
  waiting for transfers between devices  99.1 us (17%)
  between operations  19.9 us (3%)
    another operation x29, other arithmetic, sym_chol(): return jnp.linalg.cholesky(block)  160 us
    another operation x5, other arithmetic, tri_inverse(): return jax.scipy.linalg.solve_triangular(lower, eye, lower=True)  82.9 us
    all_gather x1, waiting for transfers between devices, local(): blocks = lax.all_gather(corner, ('row', 'col'), axis=0, tiled=True)  65 us
    dot_general x4, matrix products, mm_tn(): lax.dot_general(a, b, (((0,), (0,)), ((), ())), precision=HIGHEST, prefer...  45.8 us
    all_gather x1, waiting for transfers between devices, local(): rows_part = lax.all_gather(kernel[:lead_r, :], 'row', axis=0, tiled=True)  34.1 us
    transpose x1, local copies, waits for them, and re-layouts, local(): a_lead = blocks.transpose(2, 0, 3, 4, 1, 5).reshape(lead, lead)  26.1 us
    dot_general x5, matrix products, mm(): return jnp.dot(a, b, precision=HIGHEST, preferred_element_type=jnp.float32)  25.8 us
    another operation x27, local copies, waits for them, and re-layouts, tri_inverse(): return jax.scipy.linalg.solve_triangular(lower, eye, lower=True)  23.6 us
  transfers between devices with their start and end apart: 3, of which 2 were waited for; matrix products, arithmetic and copies ran while one was open for 69% of the time, Pallas kernels for 0%

commit v1 on v0

--- a/solution.py
+++ b/solution.py
@@ -56,7 +56,9 @@
     cols_part = lax.all_gather(kernel[:, :lead_c], "col", axis=1, tiled=True)
     cols_part = cols_part.reshape(rows_loc, grid_cols, lead_ct, TILE)
     x_rows = cols_part.transpose(0, 2, 1, 3).reshape(rows_loc, lead)
-    rows_part = lax.all_gather(kernel[:lead_r, :], "row", axis=0, tiled=True)
+    rows_part = jnp.concatenate(
+        lax.all_to_all(jnp.stack([kernel[:lead_r, :]] * lax.axis_size("row")), "row", 0, 0), axis=0
+    )
     rows_part = rows_part.reshape(grid_rows, lead_rt, TILE, cols_loc)
     y_cols = rows_part.transpose(1, 0, 2, 3).reshape(lead, cols_loc)
     a00 = a_lead[:PANEL, :PANEL]

time: 592 us -> 559 us (0.944)
  waiting for transfers between devices: 99.1 us -> 58.1 us
  starting transfers between devices: 0.12 us -> 6.98 us
    all_gather x1, waiting for transfers between devices: 65 us -> 8.59 us  [local(): blocks = lax.all_gather(corner, ('row', 'col'), axis=0, tiled=True)]
    all_to_all x0 -> x1, waiting for transfers between devices: none -> 49.4 us  [local(): lax.all_to_all(jnp.stack([kernel[:lead_r, :]] * lax.axis_size('row')), 'r...]
    all_gather x1 -> x0, waiting for transfers between devices: 34.1 us -> none  [local(): rows_part = lax.all_gather(kernel[:lead_r, :], 'row', axis=0, tiled=True)]
    all_to_all x0 -> x1, starting transfers between devices: none -> 6.95 us  [local(): lax.all_to_all(jnp.stack([kernel[:lead_r, :]] * lax.axis_size('row')), 'r...]
  transfers between devices with their start and end apart: 3 -> 3, of which waited for: 2 -> 2; matrix products, arithmetic and copies ran while one was open for 69% -> 73% of each run, Pallas kernels for 0% -> 0%
where the time goes in v1:
time: 559 us; the launch traced here: 552 us
  other arithmetic  260 us (47%)
  local copies, waits for them, and re-layouts  107 us (19%)
  matrix products  98.8 us (18%)
  waiting for transfers between devices  58.1 us (10%)
  between operations  20.2 us (4%)
  starting transfers between devices  6.98 us (1%)
    another operation x29, other arithmetic, sym_chol(): return jnp.linalg.cholesky(block)  160 us
    another operation x5, other arithmetic, tri_inverse(): return jax.scipy.linalg.solve_triangular(lower, eye, lower=True)  82.9 us
    all_to_all x1, waiting for transfers between devices, local(): lax.all_to_all(jnp.stack([kernel[:lead_r, :]] * lax.axis_size('row')), 'r...  49.4 us
    dot_general x4, matrix products, mm_tn(): lax.dot_general(a, b, (((0,), (0,)), ((), ())), precision=HIGHEST, prefer...  45.2 us
    transpose x1, local copies, waits for them, and re-layouts, local(): a_lead = blocks.transpose(2, 0, 3, 4, 1, 5).reshape(lead, lead)  26.1 us
    dot_general x5, matrix products, mm(): return jnp.dot(a, b, precision=HIGHEST, preferred_element_type=jnp.float32)  25.8 us
    another operation x27, local copies, waits for them, and re-layouts, tri_inverse(): return jax.scipy.linalg.solve_triangular(lower, eye, lower=True)  23.3 us
    reshape x1, local copies, waits for them, and re-layouts, local(): blocks = blocks.reshape(grid_rows, grid_cols, lead_rt, TILE, lead_ct, TILE)  16.6 us
  transfers between devices with their start and end apart: 3, of which 2 were waited for; matrix products, arithmetic and copies ran while one was open for 73% of the time, Pallas kernels for 0%

profile of v1, /device:TPU:1, one launch (start us, length us, event | category | flops | bytes accessed | tf_op | source)
XLA Modules:
  0.0 552.0 jit_solution(14065870211091037022)
XLA Ops:
  9.9 2.5 stack.2
  12.4 6.9 %all-to-all-start = ((f32[8,128,1024]{2,1,0:T(8,128)}), f32[8,128,1024]{2,1,0:T(8,128)}, u32[]{:S(2)}, u32[]{:S(2)}) async-start(f32[8,128,1024]{2,1,0:T(8,128)} %stack.2), calls=%async_computation | async-start | bytes 8388608 | tf_op jit(solution)/shard_map/all_to_all | solution.py:60
  20.7 49.4 %all-to-all-done = f32[8,128,1024]{2,1,0:T(8,128)} async-done(((f32[8,128,1024]{2,1,0:T(8,128)}), f32[8,128,1024]{2,1,0:T(8,128)}, u32[]{:S(2)}, u32[]{:S(2)}) %all-to-all-start) | async-done | bytes 4194336 | tf_op jit(solution)/shard_map/all_to_all | solution.py:60
  70.1 2.6 fusion.105
  75.7 8.6 %all-gather.6.cloned.1.call-done = f32[128,1,8192]{2,1,0:T(1,128)} async-done(((f32[1,1,8192]{2,1,0:T(1,128)}), f32[128,1,8192]{2,1,0:T(1,128)}) %all-gather.6.cloned.1.call-update) | async-done | bytes 4194320 | tf_op jit(solution)/shard_map/all_gather | solution.py:53
  84.2 13.2 %reduce.16 = f32[128,8192]{1,0:T(8,128)} reduce(f32[128,1,8192]{2,1,0:T(1,128)} %all-gather.6.cloned.1.call-done, f32[]{:T(128)} %constant.211), dimensions={1}, to_apply=%all-gather.reduce_sub_computation | reduce | bytes 8388612 | tf_op jit(solution)/shard_map/all_gather | solution.py:53
  97.5 16.6 %reshape.138 = f32[8,16,4,32,2,32]{5,4,3,2,1,0:T(2,128)} reshape(f32[128,8192]{1,0:T(8,128)} %reduce.16) | data formatting | bytes 8388608 | tf_op jit(solution)/shard_map/reshape | solution.py:54
  114.1 26.1 %copy.20 = f32[4,8,32,2,16,32]{2,1,0,5,4,3:T(8,128)} copy(f32[4,8,32,2,16,32]{5,3,2,0,4,1:T(2,128)} %bitcast.121) | data formatting | bytes 8388608 | tf_op jit(solution)/shard_map/transpose | solution.py:55
  140.2 14.2 %reshape.139 = f32[1024,1024]{0,1:T(8,128)} reshape(f32[4,8,32,2,16,32]{2,1,0,5,4,3:T(8,128)} %copy.20) | data formatting | bytes 8388608 | tf_op jit(solution)/shard_map/reshape | solution.py:55
  154.4 2.3 slice.141
  160.7 11.7 %cholesky.286 = f32[128,128]{1,0:T(8,128)S(1)} custom-call(f32[128,128]{1,0:T(8,128)S(1)} %cholesky.426), custom_call_target="Cholesky" | custom-call | tf_op jit(solution)/shard_map/jit(cholesky)/cholesky | solution.py:34
  172.4 9.8 %custom-call.27 = f32[1,128,128]{1,2,0:T(8,128)S(1)} custom-call(f32[1,128,128]{2,1,0:T(8,128)S(1)} %get-tuple-element.61), custom_call_target="InvertDiagBlocksLowerTriangular" | custom-call | tf_op jit(solution)/shard_map/jit(cholesky)/cholesky | solution.py:34
  184.9 11.7 %cholesky.305 = f32[128,128]{1,0:T(8,128)S(1)} custom-call(f32[128,128]{1,0:T(8,128)S(1)} %cholesky.430), custom_call_target="Cholesky" | custom-call | tf_op jit(solution)/shard_map/jit(cholesky)/cholesky | solution.py:34
  196.6 10.0 %custom-call.28 = f32[1,128,128]{1,2,0:T(8,128)S(1)} custom-call(f32[1,128,128]{2,1,0:T(8,128)S(1)} %get-tuple-element.58), custom_call_target="InvertDiagBlocksLowerTriangular" | custom-call | tf_op jit(solution)/shard_map/jit(cholesky)/cholesky | solution.py:34
  208.2 11.7 %cholesky.326 = f32[128,128]{1,0:T(8,128)S(1)} custom-call(f32[128,128]{1,0:T(8,128)S(1)} %cholesky.435), custom_call_target="Cholesky" | custom-call | tf_op jit(solution)/shard_map/jit(cholesky)/cholesky | solution.py:34
  219.9 9.8 %custom-call.29 = f32[1,128,128]{1,2,0:T(8,128)S(1)} custom-call(f32[1,128,128]{2,1,0:T(8,128)S(1)} %get-tuple-element.55), custom_call_target="InvertDiagBlocksLowerTriangular" | custom-call | tf_op jit(solution)/shard_map/jit(cholesky)/cholesky | solution.py:34
  231.2 11.7 %cholesky.343 = f32[128,128]{1,0:T(8,128)S(1)} custom-call(f32[128,128]{1,0:T(8,128)S(1)} %convolution_subtract_fusion.12), custom_call_target="Cholesky" | custom-call | tf_op jit(solution)/shard_map/jit(cholesky)/cholesky | solution.py:34
  249.3 11.7 %while.4 = (s32[]{:T(128)}, f32[512,512]{1,0:T(8,128)}, s32[4,2]{0,1:T(2,128)S(1)}, f32[4,128,128]{2,1,0:T(8,128)S(1)}, s32[]{:T(128)}) while((s32[]{:T(128)}, f32[512,512]{1,0:T(8,128)}, s32[4,2]{0,1:T(2,128)S(1)}, f32[4,128,128]{2,1,0:T(8,128)S(1)}, s32[]{:T(128)}) %tuple.58), condition=%wide.while_cond, body=%wide.while_body.sunk | while | flops 2 | bytes 131181 | solution.py:30
  250.0 2.3 bitcast_dynamic-update-slice_fusion.4
  252.9 2.3 bitcast_dynamic-update-slice_fusion.4
  255.8 2.3 bitcast_dynamic-update-slice_fusion.4
  258.8 2.2 bitcast_dynamic-update-slice_fusion.4
  261.0 39.3 %custom-call.30 = f32[4,128,128]{1,2,0:T(8,128)S(1)} custom-call(f32[4,128,128]{2,1,0:T(8,128)S(1)} %get-tuple-element.18), custom_call_target="InvertDiagBlocksLowerTriangular" | custom-call | tf_op jit(solution)/shard_map/jit(_solve_triangular)/triangular_solve | solution.py:30
  308.3 2.9 convolution_subtract_fusion
  311.1 2.5 copy.25
  316.5 11.7 %cholesky.358 = f32[128,128]{1,0:T(8,128)S(1)} custom-call(f32[128,128]{1,0:T(8,128)S(1)} %cholesky.439), custom_call_target="Cholesky" | custom-call | tf_op jit(solution)/shard_map/jit(cholesky)/cholesky | solution.py:34
  329.3 10.0 %custom-call.31 = f32[1,128,128]{1,2,0:T(8,128)S(1)} custom-call(f32[1,128,128]{2,1,0:T(8,128)S(1)} %get-tuple-element.51), custom_call_target="InvertDiagBlocksLowerTriangular" | custom-call | tf_op jit(solution)/shard_map/jit(cholesky)/cholesky | solution.py:34
  339.3 1.9 constant_dynamic-update-slice_fusion.3
  342.5 11.7 %cholesky.377 = f32[128,128]{1,0:T(8,128)S(1)} custom-call(f32[128,128]{1,0:T(8,128)S(1)} %cholesky.443), custom_call_target="Cholesky" | custom-call | tf_op jit(solution)/shard_map/jit(cholesky)/cholesky | solution.py:34
  354.8 9.8 %custom-call.32 = f32[1,128,128]{1,2,0:T(8,128)S(1)} custom-call(f32[1,128,128]{2,1,0:T(8,128)S(1)} %get-tuple-element.48), custom_call_target="InvertDiagBlocksLowerTriangular" | custom-call | tf_op jit(solution)/shard_map/jit(cholesky)/cholesky | solution.py:34
  367.0 11.7 %cholesky.398 = f32[128,128]{1,0:T(8,128)S(1)} custom-call(f32[128,128]{1,0:T(8,128)S(1)} %cholesky.448), custom_call_target="Cholesky" | custom-call | tf_op jit(solution)/shard_map/jit(cholesky)/cholesky | solution.py:34
  379.3 10.0 %custom-call.33 = f32[1,128,128]{1,2,0:T(8,128)S(1)} custom-call(f32[1,128,128]{2,1,0:T(8,128)S(1)} %get-tuple-element.45), custom_call_target="InvertDiagBlocksLowerTriangular" | custom-call | tf_op jit(solution)/shard_map/jit(cholesky)/cholesky | solution.py:34
  391.6 11.7 %cholesky.415 = f32[128,128]{1,0:T(8,128)S(1)} custom-call(f32[128,128]{1,0:T(8,128)S(1)} %convolution_subtract_fusion.11), custom_call_target="Cholesky" | custom-call | tf_op jit(solution)/shard_map/jit(cholesky)/cholesky | solution.py:34
  409.4 2.3 select_select_fusion
  411.7 11.7 %while.5 = (s32[]{:T(128)}, f32[512,512]{1,0:T(8,128)}, s32[4,2]{0,1:T(2,128)S(1)}, f32[4,128,128]{2,1,0:T(8,128)S(1)}, s32[]{:T(128)}) while((s32[]{:T(128)}, f32[512,512]{1,0:T(8,128)}, s32[4,2]{0,1:T(2,128)S(1)}, f32[4,128,128]{2,1,0:T(8,128)S(1)}, s32[]{:T(128)}) %tuple.68), condition=%wide.while_cond.clone, body=%wide.while_body.clone.sunk | while | flops 2 | bytes 131181 | solution.py:30
  412.4 2.2 bitcast_dynamic-update-slice_fusion.5
  415.3 2.2 bitcast_dynamic-update-slice_fusion.5
  418.3 2.2 bitcast_dynamic-update-slice_fusion.5
  421.2 2.2 bitcast_dynamic-update-slice_fusion.5
  423.4 39.7 %custom-call.34 = f32[4,128,128]{1,2,0:T(8,128)S(1)} custom-call(f32[4,128,128]{2,1,0:T(8,128)S(1)} %get-tuple-element.19), custom_call_target="InvertDiagBlocksLowerTriangular" | custom-call | tf_op jit(solution)/shard_map/jit(_solve_triangular)/triangular_solve | solution.py:30
  472.1 4.5 fusion.46
  476.6 3.5 bitcast_subtract_fusion
  480.2 5.1 convolution_select_fusion
  485.2 4.0 copy.23
  489.3 7.2 %fusion.2 = f32[512,2048]{1,0:T(8,128)S(1)} fusion(f32[1024,2048]{1,0:T(8,128)S(1)} %bitcast.122, f32[128,512]{1,0:T(8,128)S(1)} %copy-done.8, f32[128,512]{1,0:T(8,128)S(1)} %fusion.60, f32[128,512]{1,0:T(8,128)S(1)} %fusion.62, f32[128,512]{1,0:T(8,128)S(1)} %fusion.36), kind=kOutput, calls=%fused_computation.11 | convolution fusion | flops 6443237376 | bytes 9437184 | tf_op jit(solution)/shard_map/dot_general | solution.py:13
  496.4 7.2 %fusion.106 = f32[512,2048]{1,0:T(8,128)S(1)} fusion(f32[512,512]{1,0:T(8,128)S(1)} %fusion.10, f32[512,2048]{1,0:T(8,128)S(1)} %fusion.2), kind=kOutput, calls=%fused_computation.193 | convolution fusion | flops 6442450944 | bytes 9437184 | tf_op jit(solution)/shard_map/dot_general | solution.py:17
  503.6 7.2 %fusion.7 = f32[512,2048]{1,0:T(8,128)S(1)} fusion(f32[512,2048]{1,0:T(8,128)S(1)} %fusion.106, f32[1024,2048]{1,0:T(8,128)S(1)} %bitcast.123, pred[2048]{0:T(1024)(128)(4,1)S(1)} %get-tuple-element.68, f32[128,512]{1,0:T(8,128)S(1)} %fusion.53, f32[128,512]{1,0:T(8,128)S(1)} %copy-done.6, f32[128,512]{1,0:T(8,128)S(1)} %fusion.56, f32[128,512]{1,0:T(8,128)S(1)} %fusion.34), kind=kOutput, calls=%fused_computation.16 | convolution fusion | flops 6445334528 | bytes 13633536 | tf_op jit(solution)/shard_map/dot_general | solution.py:13
  513.2 31.7 %subtract_select_fusion = f32[2048,1024]{1,0:T(8,128)} fusion(f32[2048,1024]{1,0:T(8,128)} %param.4, pred[1024]{0:T(1024)(128)(4,1)S(1)} %get-tuple-element.67, pred[2048]{0:T(1024)(128)(4,1)S(1)} %get-tuple-element.69, f32[512,1024]{1,0:T(8,128)S(1)} %copy-done.11, f32[512,1024]{1,0:T(8,128)S(1)} %copy-done.3, f32[512,2048]{1,0:T(8,128)S(1)} %fusion.7, ...), kind=kOutput, calls=%fused_computation.8 | convolution fusion | flops 25779240960 | bytes 29363200 | tf_op jit(solution)/shard_map/dot_general | solution.py:17
  (116 shorter events, 59.2 us)
Async XLA Ops:
  7.2 77.1 %all-gather.6.cloned.1.call-start = ((), (), s32[]{:S(2)}) async-start(), calls=%async_computation.2 | async-start | bytes 4227072 | tf_op jit(solution)/shard_map/all_gather | solution.py:53
  12.4 7.0 %slice-start = ((f32[2048,1024]{1,0:T(8,128)}), f32[2048,64]{1,0:T(8,128)S(1)}, s32[]{:S(2)}) async-start(f32[2048,1024]{1,0:T(8,128)} %param.4), calls=%async_computation.3 | async-start | bytes 2097152 | tf_op jit(solution)/shard_map/slice | solution.py:56
  12.4 57.7 %all-to-all-start = ((f32[8,128,1024]{2,1,0:T(8,128)}), f32[8,128,1024]{2,1,0:T(8,128)}, u32[]{:S(2)}, u32[]{:S(2)}) async-start(f32[8,128,1024]{2,1,0:T(8,128)} %stack.2), calls=%async_computation | async-start | bytes 8388608 | tf_op jit(solution)/shard_map/all_to_all | solution.py:60
  19.4 465.9 %all-gather.4.cloned.1.call-start = ((), (), s32[]{:S(2)}) async-start(), calls=%async_computation.1 | async-start | bytes 8912896 | tf_op jit(solution)/shard_map/all_gather | solution.py:56
  159.7 1.0 copy-start.10
  300.3 6.1 %copy-start = (f32[1024,1024]{0,1:T(8,128)S(1)}, f32[1024,1024]{0,1:T(8,128)}, u32[]{:S(2)}) copy-start(f32[1024,1024]{0,1:T(8,128)} %reshape.139) | copy-start | bytes 12582916
  306.4 7.3 %copy-start.7 = (f32[128,512]{1,0:T(8,128)}, f32[128,512]{1,0:T(8,128)S(1)}, u32[]{:S(2)}) copy-start(f32[128,512]{1,0:T(8,128)S(1)} %fusion.59) | copy-start | bytes 786436
  315.5 1.0 copy-start.9
  463.1 0.7 copy-start.12
  463.2 8.9 %copy-start.4 = (f32[2,8,32,1024]{3,2,1,0:T(8,128)S(1)}, f32[2,8,32,1024]{3,2,1,0:T(8,128)}, u32[]{:S(2)}) copy-start(f32[2,8,32,1024]{3,2,1,0:T(8,128)} %copy.26) | copy-start | bytes 6291460
  467.7 8.9 %copy-start.1 = (f32[2,8,32,1024]{3,2,1,0:T(8,128)S(1)}, f32[2,8,32,1024]{3,2,1,0:T(8,128)}, u32[]{:S(2)}) copy-start(f32[2,8,32,1024]{3,2,1,0:T(8,128)} %copy.27) | copy-start | bytes 6291460
  469.1 11.1 %copy-start.5 = (f32[128,512]{1,0:T(8,128)}, f32[128,512]{1,0:T(8,128)S(1)}, u32[]{:S(2)}) copy-start(f32[128,512]{1,0:T(8,128)S(1)} %fusion.54) | copy-start | bytes 786436
  476.6 3.5 copy-start.2
  485.2 4.0 copy-start.8
  496.4 7.2 %copy-start.6 = (f32[128,512]{1,0:T(8,128)S(1)}, f32[128,512]{1,0:T(8,128)}, u32[]{:S(2)}) copy-start(f32[128,512]{1,0:T(8,128)} %copy-done.5) | copy-start | bytes 786436
  510.8 1.8 copy-start.3
  510.8 2.4 copy-start.11
Sparse Core Ops, SparseCore 0:
  11.1 73.0 all-gather.5
  87.0 67.5 all-gather.3
